TPU v7x, 32 devices: a whole 2x2x4 slice. The times are simulated.
32 devices in a mesh: dp: 2 (over y), expert: 16 (over z, x, core).
Axes of the slice: x: 2, y: 2, z: 4, core: 2. Of those that a mesh axis runs over, the one named last changes fastest.
Arguments:
- tokens: bfloat16 [4096, 2048], P(('dp', 'expert')), may hold values from -6 to 6
- grad_out: bfloat16 [4096, 2048], P(('dp', 'expert')), may hold values from -6 to 6
- expert_ids: int32 [4096, 8], P(('dp', 'expert')), may hold values from 0 to 15, all different within a row; in each aligned block of 128 rows (0 to 127, 128 to 255, ...) at most 72 rows name the same one
- route_weight: bfloat16 [4096, 8], P(('dp', 'expert')), may hold values from 0.049804688 to 1
- w_gate: bfloat16 [16, 2048, 384], P('expert', 'dp'), may hold values from -0.125 to 0.125
- w_up: bfloat16 [16, 2048, 384], P('expert', 'dp'), may hold values from -0.125 to 0.125
- w_down: bfloat16 [16, 384, 2048], P('expert', None, 'dp'), may hold values from -0.3125 to 0.3125
Outputs:
- grad_tokens: bfloat16 [4096, 2048], P(('dp', 'expert'))
- grad_route: bfloat16 [4096, 8], P(('dp', 'expert'))
Inputs may be any that keep to these rules, and one draw needn't show every extreme that they name: `expert_ids`: each row names 8 different experts; among the 128 rows of one device no expert is named by more than 72 rows, and in every draw some expert is named by exactly 72 rows of some device.
All inputs are finite; a program needn't handle non-finite values.
Results may differ from a plain program's by a relative error of at most 0.012.
Values may be sent and summed in bfloat16 or wider, within the bound.
A program may use at most 128 MiB of HBM per device.

v0:
```python
import jax
import jax.numpy as jnp
from jax import lax
from jax.sharding import PartitionSpec as P


def expert_rows(x_rows, g_rows, weight_rows, gate_mat, up_mat, down_mat):
    gate_pre = jnp.dot(x_rows, gate_mat, preferred_element_type=jnp.float32)
    up_pre = jnp.dot(x_rows, up_mat, preferred_element_type=jnp.float32)
    sigmoid_gate = jax.nn.sigmoid(gate_pre)
    active = gate_pre * sigmoid_gate
    hidden = active * up_pre
    back_hidden = jnp.dot(g_rows, down_mat.T, preferred_element_type=jnp.float32)
    route_grad = jnp.sum(hidden * back_hidden, axis=1)
    scaled = weight_rows.astype(jnp.float32)[:, None] * back_hidden
    slope = sigmoid_gate * (1.0 + gate_pre * (1.0 - sigmoid_gate))
    d_gate = (scaled * up_pre * slope).astype(jnp.bfloat16)
    d_up = (scaled * active).astype(jnp.bfloat16)
    input_grad = jnp.dot(d_gate, gate_mat.T, preferred_element_type=jnp.float32) + jnp.dot(
        d_up, up_mat.T, preferred_element_type=jnp.float32
    )
    return (input_grad.astype(jnp.bfloat16), route_grad.astype(jnp.bfloat16))


def per_device(tokens, grad_out, expert_ids, route_weight, w_gate, w_up, w_down):
    tok_rows, width_model = tokens.shape
    n_expert = lax.axis_size("expert")
    gate_mat, up_mat, down_mat = (
        lax.all_gather(w_gate[0], "dp", axis=0, tiled=True),
        lax.all_gather(w_up[0], "dp", axis=0, tiled=True),
        lax.all_gather(w_down[0], "dp", axis=1, tiled=True),
    )
    chosen = expert_ids[:, :, None] == jnp.arange(n_expert, dtype=jnp.int32)[None, None, :]
    dense_w = jnp.sum(
        jnp.where(chosen, route_weight[:, :, None].astype(jnp.float32), 0.0), axis=1
    ).astype(jnp.bfloat16)
    weight_rows = lax.all_to_all(dense_w.T, "expert", split_axis=0, concat_axis=0, tiled=True)
    all_x = lax.all_gather(tokens, "expert", axis=0, tiled=True)
    all_g = lax.all_gather(grad_out, "expert", axis=0, tiled=True)
    out_grad, out_route = expert_rows(
        all_x, all_g, weight_rows.reshape(-1), gate_mat, up_mat, down_mat
    )
    grad_tokens = lax.psum_scatter(out_grad, "expert", scatter_dimension=0, tiled=True)
    back_route = lax.all_to_all(
        out_route.reshape(n_expert, tok_rows), "expert", split_axis=0, concat_axis=0, tiled=True
    )
    grad_route = jnp.sum(
        jnp.where(chosen, back_route.T[:, None, :].astype(jnp.float32), 0.0), axis=2
    ).astype(jnp.bfloat16)
    return (grad_tokens, grad_route)


def solution(mesh):
    return jax.shard_map(
        per_device,
        mesh=mesh,
        in_specs=(
            P(("dp", "expert"), None),
            P(("dp", "expert"), None),
            P(("dp", "expert"), None),
            P(("dp", "expert"), None),
            P("expert", "dp", None),
            P("expert", "dp", None),
            P("expert", None, "dp"),
        ),
        out_specs=(P(("dp", "expert"), None), P(("dp", "expert"), None)),
        check_vma=False,
    )
```

profile of v0, /device:TPU:0, one launch (start us, length us, event | category | flops | bytes accessed | tf_op | source)
XLA Modules:
  0.0 415.4 jit_solution(4736880149228869505)
XLA Ops:
  7.2 0.0 all-gather.17.cloned.1.call-start
  7.2 0.7 all-gather.17.cloned.1.call-update
  7.9 0.0 all-gather.11.cloned.1.call-start
  7.9 0.7 all-gather.11.cloned.1.call-update
  8.6 0.0 all-gather.15.cloned.1.call-start
  8.7 0.7 all-gather.15.cloned.1.call-update
  9.4 0.0 all-gather.13.cloned.1.call-start
  9.4 0.5 all-gather.13.cloned.1.call-update
  10.0 0.0 all-gather.9.cloned.1.call-start
  10.0 0.5 all-gather.9.cloned.1.call-update
  10.5 28.9 %all-gather.17.cloned.1.call-done = bf16[1,2048,384]{2,1,0:T(8,128)(2,1)} async-done(((bf16[1,1024,384]{2,1,0:T(8,128)(2,1)}), bf16[1,2048,384]{2,1,0:T(8,128)(2,1)}) %all-gather.17.cloned.1.call-update) | async-done | bytes 1572880 | tf_op jit(solution)/shard_map/all_gather | solution.py:29
  39.5 76.5 %all-gather.11.cloned.1.call-done = bf16[2048,2048]{1,0:T(8,128)(2,1)} async-done(((bf16[128,2048]{1,0:T(8,128)(2,1)}), bf16[2048,2048]{1,0:T(8,128)(2,1)}) %all-gather.11.cloned.1.call-update) | async-done | bytes 8388624 | tf_op jit(solution)/shard_map/all_gather | solution.py:38
  115.9 6.4 %fusion.3 = f32[2048,384]{0,1:T(8,128)S(1)} fusion(bf16[2048,2048]{1,0:T(8,128)(2,1)} %all-gather.11.cloned.1.call-done, bf16[1,2048,384]{2,1,0:T(8,128)(2,1)} %all-gather.17.cloned.1.call-done), kind=kOutput, calls=%fused_computation.8 | convolution fusion | flops 3221225472 | bytes 13107200 | tf_op jit(solution)/shard_map/dot_general | solution.py:8
  122.3 21.0 %all-gather.15.cloned.1.call-done = bf16[1,2048,384]{2,1,0:T(8,128)(2,1)} async-done(((bf16[1,1024,384]{2,1,0:T(8,128)(2,1)}), bf16[1,2048,384]{2,1,0:T(8,128)(2,1)}) %all-gather.15.cloned.1.call-update) | async-done | bytes 1572880 | tf_op jit(solution)/shard_map/all_gather | solution.py:30
  143.3 8.9 %fusion.6 = f32[2048,384]{0,1:T(8,128)} fusion(bf16[2048,2048]{1,0:T(8,128)(2,1)} %all-gather.11.cloned.1.call-done, bf16[1,2048,384]{2,1,0:T(8,128)(2,1)} %all-gather.15.cloned.1.call-done), kind=kOutput, calls=%fused_computation.11 | convolution fusion | flops 3221225472 | bytes 13107200 | tf_op jit(solution)/shard_map/dot_general | solution.py:9
  152.2 0.0 copy-start.1
  152.2 0.0 copy-start
  152.2 19.7 %all-gather.13.cloned.1.call-done = bf16[1,384,2048]{2,1,0:T(8,128)(2,1)} async-done(((bf16[1,384,1024]{2,1,0:T(8,128)(2,1)}), bf16[1,384,2048]{2,1,0:T(8,128)(2,1)}) %all-gather.13.cloned.1.call-update) | async-done | bytes 1572880 | tf_op jit(solution)/shard_map/all_gather | solution.py:31
  171.9 76.3 %all-gather.9.cloned.1.call-done = bf16[2048,2048]{1,0:T(8,128)(2,1)} async-done(((bf16[128,2048]{1,0:T(8,128)(2,1)}), bf16[2048,2048]{1,0:T(8,128)(2,1)}) %all-gather.9.cloned.1.call-update) | async-done | bytes 8388624 | tf_op jit(solution)/shard_map/all_gather | solution.py:39
  248.2 10.1 %multiply_reduce_fusion = (bf16[2048]{0:T(1024)(128)(2,1)S(1)}, f32[2048,384]{0,1:T(8,128)}) fusion(f32[2048,384]{0,1:T(8,128)} %fusion.6, f32[2048,384]{0,1:T(8,128)S(1)} %fusion.3, bf16[2048,2048]{1,0:T(8,128)(2,1)} %all-gather.9.cloned.1.call-done, bf16[1,384,2048]{2,1,0:T(8,128)(2,1)} %all-gather.13.cloned.1.call-done), kind=kOutput, calls=%fused_computation.1 | convolution fusion | flops 3226728448 | bytes 19402752 | tf_op jit(solution)/shard_map/dot_general | solution.py:13
  258.3 0.6 copy.27
  258.9 3.5 all-to-all-start.1
  262.4 0.0 reduce-scatter.2.cloned.1.call-start
  262.5 0.0 copy-done.1
  262.5 6.3 %all-to-all-done.1 = bf16[16,1,128]{2,1,0:T(2,128)(2,1)S(1)} async-done(((bf16[16,1,128]{2,1,0:T(2,128)(2,1)}), bf16[16,1,128]{2,1,0:T(2,128)(2,1)S(1)}, u32[]{:S(2)}, u32[]{:S(2)}) %all-to-all-start.1) | async-done | bytes 4128 | tf_op jit(solution)/shard_map/all_to_all | solution.py:44
  268.7 0.0 copy-done
  268.8 0.6 select_reduce_fusion
  269.4 9.0 %all_to_all.15 = bf16[16,1,128]{2,1,0:T(2,128)(2,1)S(1)} all-to-all(bf16[16,1,128]{2,1,0:T(2,128)(2,1)S(1)} %copy.25), channel_id=1, replica_groups=mesh['dp'=2,'expert'=16] {'expert'}, dimensions={0} | all-to-all | bytes 8192 | tf_op jit(solution)/shard_map/all_to_all | solution.py:37
  278.4 14.2 %fusion.1 = f32[2048,2048]{1,0:T(8,128)} fusion(f32[2048,384]{0,1:T(8,128)S(1)} %fusion.3, f32[2048,384]{0,1:T(8,128)} %fusion.6, f32[2048,384]{0,1:T(8,128)} %get-tuple-element.5, bf16[1,2048,384]{2,1,0:T(8,128)(2,1)} %all-gather.17.cloned.1.call-done, f32[2048]{0:T(1024)S(1)} %bitcast_convert_fusion), kind=kOutput, calls=%fused_computation.6 | convolution fusion | flops 3229876224 | bytes 27795456 | tf_op jit(solution)/shard_map/dot_general | solution.py:19
  292.6 15.1 %add_convert_fusion = bf16[2048,2048]{1,0:T(8,128)(2,1)} fusion(f32[2048,2048]{1,0:T(8,128)} %fusion.1, f32[2048,384]{0,1:T(8,128)} %get-tuple-element.5, bf16[1,2048,384]{2,1,0:T(8,128)(2,1)} %all-gather.15.cloned.1.call-done, f32[2048]{0:T(1024)S(1)} %bitcast_convert_fusion, f32[2048,384]{0,1:T(8,128)S(1)} %fusion.3), kind=kOutput, calls=%fused_computation | convolution fusion | flops 3235119104 | bytes 33038336 | tf_op jit(solution)/shard_map/dot_general | solution.py:19
  307.7 0.0 reduce-scatter.2.cloned.1.call-update
  307.7 100.8 %reduce-scatter.2.cloned.1.call-done = bf16[128,2048]{1,0:T(8,128)(2,1)} async-done(((bf16[2048,2048]{1,0:T(8,128)(2,1)}), bf16[128,2048]{1,0:T(8,128)(2,1)}) %reduce-scatter.2.cloned.1.call-update) | async-done | bytes 524304 | tf_op jit(solution)/shard_map/reduce_scatter | solution.py:43
  (4 shorter events, 0.0 us)
Async XLA Ops:
  7.2 32.3 %all-gather.17.cloned.1.call-start = ((), (), s32[]{:S(2)}) async-start(), calls=%async_computation.8 | async-start | bytes 2359296 | tf_op jit(solution)/shard_map/all_gather | solution.py:29
  7.9 108.0 %all-gather.11.cloned.1.call-start = ((), (), s32[]{:S(2)}) async-start(), calls=%async_computation.4 | async-start | bytes 8912896 | tf_op jit(solution)/shard_map/all_gather | solution.py:38
  8.6 134.6 %all-gather.15.cloned.1.call-start = ((), (), s32[]{:S(2)}) async-start(), calls=%async_computation.7 | async-start | bytes 2359296 | tf_op jit(solution)/shard_map/all_gather | solution.py:30
  9.4 162.5 %all-gather.13.cloned.1.call-start = ((), (), s32[]{:S(2)}) async-start(), calls=%async_computation.6 | async-start | bytes 2359296 | tf_op jit(solution)/shard_map/all_gather | solution.py:31
  10.0 238.3 %all-gather.9.cloned.1.call-start = ((), (), s32[]{:S(2)}) async-start(), calls=%async_computation.3 | async-start | bytes 8912896 | tf_op jit(solution)/shard_map/all_gather | solution.py:39
  152.2 110.3 %copy-start.1 = (bf16[128,8]{0,1:T(8,128)(2,1)S(1)}, bf16[128,8]{0,1:T(8,128)(2,1)}, u32[]{:S(2)}) copy-start(bf16[128,8]{0,1:T(8,128)(2,1)} %param.10) | copy-start | bytes 6148
  152.2 116.5 %copy-start = (s32[128,8]{0,1:T(8,128)S(1)}, s32[128,8]{0,1:T(8,128)}, u32[]{:S(2)}) copy-start(s32[128,8]{0,1:T(8,128)} %param.9) | copy-start | bytes 12292
  258.9 9.8 %all-to-all-start.1 = ((bf16[16,1,128]{2,1,0:T(2,128)(2,1)}), bf16[16,1,128]{2,1,0:T(2,128)(2,1)S(1)}, u32[]{:S(2)}, u32[]{:S(2)}) async-start(bf16[16,1,128]{2,1,0:T(2,128)(2,1)} %copy.27), calls=%async_computation.2 | async-start | bytes 16384 | tf_op jit(solution)/shard_map/all_to_all | solution.py:44
  262.4 146.1 %reduce-scatter.2.cloned.1.call-start = ((), (), s32[]{:S(2)}) async-start(), calls=%async_computation.5 | async-start | bytes 8912896 | tf_op jit(solution)/shard_map/reduce_scatter | solution.py:43
Sparse Core Ops, SparseCore 0:
  9.5 29.8 all-gather.16
  41.6 74.2 all-gather.10
  117.5 25.7 all-gather.14
  144.7 27.1 all-gather.12
  173.9 74.2 all-gather.8
  307.8 100.6 reduce-scatter.1
where the time goes:
time: 416 us; the launch traced here: 415 us
  waiting for transfers between devices  333 us (80%)
  matrix products  54.6 us (13%)
  between operations  14.2 us (3%)
  blocking collectives  8.99 us (2%)
    reduce_scatter x1, waiting for transfers between devices, per_device(): lax.psum_scatter(out_grad, 'expert', scatter_dimension=0, tiled=True)  101 us
    all_gather x1, waiting for transfers between devices, per_device(): all_x = lax.all_gather(tokens, 'expert', axis=0, tiled=True)  76.5 us
    all_gather x1, waiting for transfers between devices, per_device(): all_g = lax.all_gather(grad_out, 'expert', axis=0, tiled=True)  76.3 us
    all_gather x1, waiting for transfers between devices, per_device(): lax.all_gather(w_gate[0], 'dp', axis=0, tiled=True)  28.9 us
    all_gather x1, waiting for transfers between devices, per_device(): lax.all_gather(w_up[0], 'dp', axis=0, tiled=True)  21 us
    all_gather x1, waiting for transfers between devices, per_device(): lax.all_gather(w_down[0], 'dp', axis=1, tiled=True)  19.7 us
    dot_general x1, matrix products, expert_rows(): jnp.dot(d_up, up_mat.T, preferred_element_type=jnp.float32)  15.1 us
    dot_general x1, matrix products, expert_rows(): jnp.dot(d_gate, gate_mat.T, preferred_element_type=jnp.float32)  14.2 us
  transfers between devices with their start and end apart: 7, of which 7 were waited for; matrix products, arithmetic and copies ran while one was open for 4% of the time, Pallas kernels for 0%

commit v1 on v0

--- a/solution.py
+++ b/solution.py
@@ -35,8 +35,11 @@
         jnp.where(chosen, route_weight[:, :, None].astype(jnp.float32), 0.0), axis=1
     ).astype(jnp.bfloat16)
     weight_rows = lax.all_to_all(dense_w.T, "expert", split_axis=0, concat_axis=0, tiled=True)
-    all_x = lax.all_gather(tokens, "expert", axis=0, tiled=True)
-    all_g = lax.all_gather(grad_out, "expert", axis=0, tiled=True)
+    all_x, all_g = jnp.split(
+        lax.all_gather(jnp.concatenate([tokens, grad_out], axis=1), "expert", axis=0, tiled=True),
+        [tokens.shape[1]],
+        axis=1,
+    )
     out_grad, out_route = expert_rows(
         all_x, all_g, weight_rows.reshape(-1), gate_mat, up_mat, down_mat
     )

time: 416 us -> 392 us (0.942)
  waiting for transfers between devices: 333 us -> 305 us
    all_gather x2 -> x1, waiting for transfers between devices: 153 us -> 129 us  [per_device(): lax.all_gather(jnp.concatenate([tokens, grad_out], axis=1), 'expert', axi...]
  transfers between devices with their start and end apart: 7 -> 6, of which waited for: 7 -> 6; matrix products, arithmetic and copies ran while one was open for 4% -> 4% of each run, Pallas kernels for 0% -> 0%
where the time goes in v1:
time: 392 us
  waiting for transfers between devices  305 us (78%)
  matrix products  54.6 us (14%)
  between operations  13.8 us (4%)
  blocking collectives  8.99 us (2%)
  starting transfers between devices  5.82 us (1%)
    all_gather x1, waiting for transfers between devices, per_device(): lax.all_gather(jnp.concatenate([tokens, grad_out], axis=1), 'expert', axi...  129 us
    reduce_scatter x1, waiting for transfers between devices, per_device(): lax.psum_scatter(out_grad, 'expert', scatter_dimension=0, tiled=True)  99.9 us
    all_gather x1, waiting for transfers between devices, per_device(): lax.all_gather(w_gate[0], 'dp', axis=0, tiled=True)  27.9 us
    all_gather x1, waiting for transfers between devices, per_device(): lax.all_gather(w_up[0], 'dp', axis=0, tiled=True)  20.6 us
    all_gather x1, waiting for transfers between devices, per_device(): lax.all_gather(w_down[0], 'dp', axis=1, tiled=True)  19.7 us
    dot_general x1, matrix products, expert_rows(): jnp.dot(d_up, up_mat.T, preferred_element_type=jnp.float32)  15.1 us
    dot_general x1, matrix products, expert_rows(): jnp.dot(d_gate, gate_mat.T, preferred_element_type=jnp.float32)  14.2 us
    dot_general x1, matrix products, expert_rows(): jnp.dot(g_rows, down_mat.T, preferred_element_type=jnp.float32)  10.1 us
  transfers between devices with their start and end apart: 6, of which 6 were waited for; matrix products, arithmetic and copies ran while one was open for 4% of the time, Pallas kernels for 0%

profile of v1, /device:TPU:0, one launch (start us, length us, event | category | flops | bytes accessed | tf_op | source)
XLA Modules:
  0.0 391.7 jit_solution(16998676901793406140)
XLA Ops:
  7.2 0.0 all-gather.14.cloned.1.call-start
  7.2 0.7 all-gather.14.cloned.1.call-update
  7.9 0.0 all-gather.8.cloned.1.call-start
  7.9 2.3 pad_maximum_fusion
  10.2 0.0 all-gather.8.cloned.1.call-update
  10.2 0.0 all-gather.12.cloned.1.call-start
  10.3 0.7 all-gather.12.cloned.1.call-update
  11.0 0.0 all-gather.10.cloned.1.call-start
  11.0 0.5 all-gather.10.cloned.1.call-update
  11.6 27.9 %all-gather.14.cloned.1.call-done = bf16[1,2048,384]{2,1,0:T(8,128)(2,1)} async-done(((bf16[1,1024,384]{2,1,0:T(8,128)(2,1)}), bf16[1,2048,384]{2,1,0:T(8,128)(2,1)}) %all-gather.14.cloned.1.call-update) | async-done | bytes 1572880 | tf_op jit(solution)/shard_map/all_gather | solution.py:29
  39.5 128.6 %all-gather.8.cloned.1.call-done = bf16[2048,4096]{1,0:T(8,128)(2,1)} async-done(((bf16[128,4096]{1,0:T(8,128)(2,1)}), bf16[2048,4096]{1,0:T(8,128)(2,1)}) %all-gather.8.cloned.1.call-update) | async-done | bytes 16777232 | tf_op jit(solution)/shard_map/all_gather | solution.py:39
  168.1 6.4 %fusion.2 = f32[2048,384]{0,1:T(8,128)S(1)} fusion(bf16[2048,4096]{1,0:T(8,128)(2,1)} %all-gather.8.cloned.1.call-done, bf16[1,2048,384]{2,1,0:T(8,128)(2,1)} %all-gather.14.cloned.1.call-done), kind=kOutput, calls=%fused_computation.3 | convolution fusion | flops 3221225472 | bytes 13107200 | tf_op jit(solution)/shard_map/dot_general | solution.py:8
  174.4 20.6 %all-gather.12.cloned.1.call-done = bf16[1,2048,384]{2,1,0:T(8,128)(2,1)} async-done(((bf16[1,1024,384]{2,1,0:T(8,128)(2,1)}), bf16[1,2048,384]{2,1,0:T(8,128)(2,1)}) %all-gather.12.cloned.1.call-update) | async-done | bytes 1572880 | tf_op jit(solution)/shard_map/all_gather | solution.py:30
  195.0 8.9 %fusion.4 = f32[2048,384]{0,1:T(8,128)} fusion(bf16[2048,4096]{1,0:T(8,128)(2,1)} %all-gather.8.cloned.1.call-done, bf16[1,2048,384]{2,1,0:T(8,128)(2,1)} %all-gather.12.cloned.1.call-done), kind=kOutput, calls=%fused_computation.5 | convolution fusion | flops 3221225472 | bytes 13107200 | tf_op jit(solution)/shard_map/dot_general | solution.py:9
  203.9 0.0 copy-start.1
  203.9 0.0 copy-start
  203.9 19.7 %all-gather.10.cloned.1.call-done = bf16[1,384,2048]{2,1,0:T(8,128)(2,1)} async-done(((bf16[1,384,1024]{2,1,0:T(8,128)(2,1)}), bf16[1,384,2048]{2,1,0:T(8,128)(2,1)}) %all-gather.10.cloned.1.call-update) | async-done | bytes 1572880 | tf_op jit(solution)/shard_map/all_gather | solution.py:31
  223.6 10.1 %multiply_reduce_fusion = (bf16[2048]{0:T(1024)(128)(2,1)S(1)}, f32[2048,384]{0,1:T(8,128)}) fusion(f32[2048,384]{0,1:T(8,128)} %fusion.4, f32[2048,384]{0,1:T(8,128)S(1)} %fusion.2, bf16[1,384,2048]{2,1,0:T(8,128)(2,1)} %all-gather.10.cloned.1.call-done, bf16[2048,4096]{1,0:T(8,128)(2,1)} %all-gather.8.cloned.1.call-done), kind=kOutput, calls=%fused_computation.7 | convolution fusion | flops 3226728448 | bytes 19402752 | tf_op jit(solution)/shard_map/dot_general | solution.py:13
  233.7 0.6 copy.27
  234.3 5.6 %all-to-all-start.1 = ((bf16[16,1,128]{2,1,0:T(2,128)(2,1)}), bf16[16,1,128]{2,1,0:T(2,128)(2,1)S(1)}, u32[]{:S(2)}, u32[]{:S(2)}) async-start(bf16[16,1,128]{2,1,0:T(2,128)(2,1)} %copy.27), calls=%async_computation.2 | async-start | bytes 16384 | tf_op jit(solution)/shard_map/all_to_all | solution.py:47
  240.0 0.0 reduce-scatter.2.cloned.1.call-start
  240.0 0.0 copy-done.1
  240.0 6.3 %all-to-all-done.1 = bf16[16,1,128]{2,1,0:T(2,128)(2,1)S(1)} async-done(((bf16[16,1,128]{2,1,0:T(2,128)(2,1)}), bf16[16,1,128]{2,1,0:T(2,128)(2,1)S(1)}, u32[]{:S(2)}, u32[]{:S(2)}) %all-to-all-start.1) | async-done | bytes 4128 | tf_op jit(solution)/shard_map/all_to_all | solution.py:47
  246.3 0.0 copy-done
  246.3 0.6 select_reduce_fusion
  247.0 9.0 %all_to_all.15 = bf16[16,1,128]{2,1,0:T(2,128)(2,1)S(1)} all-to-all(bf16[16,1,128]{2,1,0:T(2,128)(2,1)S(1)} %copy.25), channel_id=1, replica_groups=mesh['dp'=2,'expert'=16] {'expert'}, dimensions={0} | all-to-all | bytes 8192 | tf_op jit(solution)/shard_map/all_to_all | solution.py:37
  256.0 14.2 %fusion.7 = f32[2048,2048]{1,0:T(8,128)} fusion(f32[2048,384]{0,1:T(8,128)S(1)} %fusion.2, f32[2048,384]{0,1:T(8,128)} %fusion.4, f32[2048,384]{0,1:T(8,128)} %get-tuple-element.5, bf16[1,2048,384]{2,1,0:T(8,128)(2,1)} %all-gather.14.cloned.1.call-done, f32[2048]{0:T(1024)S(1)} %bitcast_convert_fusion), kind=kOutput, calls=%fused_computation.12 | convolution fusion | flops 3229876224 | bytes 27795456 | tf_op jit(solution)/shard_map/dot_general | solution.py:19
  270.2 15.1 %add_convert_fusion = bf16[2048,2048]{1,0:T(8,128)(2,1)} fusion(f32[2048,2048]{1,0:T(8,128)} %fusion.7, f32[2048,384]{0,1:T(8,128)} %get-tuple-element.5, bf16[1,2048,384]{2,1,0:T(8,128)(2,1)} %all-gather.12.cloned.1.call-done, f32[2048]{0:T(1024)S(1)} %bitcast_convert_fusion, f32[2048,384]{0,1:T(8,128)S(1)} %fusion.2), kind=kOutput, calls=%fused_computation | convolution fusion | flops 3235119104 | bytes 33038336 | tf_op jit(solution)/shard_map/dot_general | solution.py:19
  285.3 0.0 reduce-scatter.2.cloned.1.call-update
  285.3 99.9 %reduce-scatter.2.cloned.1.call-done = bf16[128,2048]{1,0:T(8,128)(2,1)} async-done(((bf16[2048,2048]{1,0:T(8,128)(2,1)}), bf16[128,2048]{1,0:T(8,128)(2,1)}) %reduce-scatter.2.cloned.1.call-update) | async-done | bytes 524304 | tf_op jit(solution)/shard_map/reduce_scatter | solution.py:46
  (4 shorter events, 0.0 us)
Async XLA Ops:
  7.2 32.3 %all-gather.14.cloned.1.call-start = ((), (), s32[]{:S(2)}) async-start(), calls=%async_computation.7 | async-start | bytes 2359296 | tf_op jit(solution)/shard_map/all_gather | solution.py:29
  7.9 160.2 %all-gather.8.cloned.1.call-start = ((), (), s32[]{:S(2)}) async-start(), calls=%async_computation.3 | async-start | bytes 17825792 | tf_op jit(solution)/shard_map/all_gather | solution.py:39
  10.2 184.8 %all-gather.12.cloned.1.call-start = ((), (), s32[]{:S(2)}) async-start(), calls=%async_computation.6 | async-start | bytes 2359296 | tf_op jit(solution)/shard_map/all_gather | solution.py:30
  11.0 212.7 %all-gather.10.cloned.1.call-start = ((), (), s32[]{:S(2)}) async-start(), calls=%async_computation.5 | async-start | bytes 2359296 | tf_op jit(solution)/shard_map/all_gather | solution.py:31
  203.9 36.1 %copy-start.1 = (bf16[128,8]{0,1:T(8,128)(2,1)S(1)}, bf16[128,8]{0,1:T(8,128)(2,1)}, u32[]{:S(2)}) copy-start(bf16[128,8]{0,1:T(8,128)(2,1)} %param.10) | copy-start | bytes 6148
  203.9 42.4 %copy-start = (s32[128,8]{0,1:T(8,128)S(1)}, s32[128,8]{0,1:T(8,128)}, u32[]{:S(2)}) copy-start(s32[128,8]{0,1:T(8,128)} %param.9) | copy-start | bytes 12292
  234.3 12.0 %all-to-all-start.1 = ((bf16[16,1,128]{2,1,0:T(2,128)(2,1)}), bf16[16,1,128]{2,1,0:T(2,128)(2,1)S(1)}, u32[]{:S(2)}, u32[]{:S(2)}) async-start(bf16[16,1,128]{2,1,0:T(2,128)(2,1)} %copy.27), calls=%async_computation.2 | async-start | bytes 16384 | tf_op jit(solution)/shard_map/all_to_all | solution.py:47
  240.0 145.2 %reduce-scatter.2.cloned.1.call-start = ((), (), s32[]{:S(2)}) async-start(), calls=%async_computation.4 | async-start | bytes 8912896 | tf_op jit(solution)/shard_map/reduce_scatter | solution.py:46
Sparse Core Ops, SparseCore 0:
  9.5 29.9 all-gather.13
  41.6 126.4 all-gather.7
  169.6 25.3 all-gather.11
  196.4 27.1 all-gather.9
  285.4 99.7 reduce-scatter.1
